TPU v7x, 256 devices: a whole 4x4x8 slice. The times are simulated.
256 devices in a mesh: rows: 64 (over z, y, core), grp: 4 (over x).
Axes of the slice: x: 4, y: 4, z: 8, core: 2. Of those that a mesh axis runs over, the one named last changes fastest.
Arguments:
- matrix: float32 [524288, 512], P(('rows', 'grp')), may hold values from -6 to 6
- sign_bits: int32 [524288], P(('rows', 'grp')), may hold values from 0 to 1
- samples: int32 [16, 16384], P('grp'), may hold values from 0 to 32767, as said below
Outputs:
- r_factor: float32 [512, 512], replicated
- solved: float32 [524288, 512], P(('rows', 'grp'))
Inputs may be any that keep to these rules, and one draw needn't show every extreme that they name: `samples`: each row names 16384 distinct positions of a batch, exactly one of each pair 2 k and 2 k + 1, in any order.
All inputs are finite; a program needn't handle non-finite values.
Results may differ from a plain program's by a relative error of at most 0.0001.
Values sent between devices are 32-bit elements; how exact they have to be, the bound alone decides.
No kernel may reach another device: no remote copies, remote signals or barrier semaphores. Data moves between devices by JAX's collectives and lax.ppermute only.
A program may use at most 128 MiB of HBM per device.

v0:
```python
import jax
import jax.numpy as jnp
from jax import lax
from jax.sharding import PartitionSpec as P

INNER = 256


def cosine_sorted(size):
    evens = jnp.arange(0, size, 2, dtype=jnp.int32)
    odds = jnp.arange(1, size, 2, dtype=jnp.int32)
    freq = jnp.concatenate([evens, odds])[:, None]
    place = jnp.arange(size, dtype=jnp.int32)[None, :]
    phase = (2 * place + 1) * freq % (4 * size)
    weight = jnp.where(freq == 0, 1.0, 2.0).astype(jnp.float32) / size
    return jnp.sqrt(weight) * jnp.cos(jnp.pi * phase.astype(jnp.float32) / (2 * size))


def cosine(size):
    freq = jnp.arange(size, dtype=jnp.int32)[:, None]
    place = jnp.arange(size, dtype=jnp.int32)[None, :]
    phase = (2 * place + 1) * freq % (4 * size)
    weight = jnp.where(freq == 0, 1.0, 2.0).astype(jnp.float32) / size
    return jnp.sqrt(weight) * jnp.cos(jnp.pi * phase.astype(jnp.float32) / (2 * size))


def pair_parity(chosen):
    return jnp.zeros(chosen.shape, jnp.int32).at[chosen // 2].set(chosen % 2)


def local(matrix, sign_bits, samples):
    nrows = lax.axis_size("rows")
    ngroups = lax.axis_size("grp")
    batches, half = samples.shape
    per_device = matrix.shape[0] // batches
    width = matrix.shape[1]
    narrow = width // nrows
    total = per_device * nrows
    outer = total // INNER
    halfin = INNER // 2
    signed = matrix * (1 - 2 * sign_bits).astype(jnp.float32)[:, None]
    local_rows = signed.reshape(batches, per_device // INNER, INNER, width)
    c_inner = cosine_sorted(INNER)
    c_outer = cosine(outer)
    first = jnp.einsum("qp,bspn->bnsq", c_inner, local_rows, precision=lax.Precision.HIGHEST)
    first = first.reshape(batches, width, per_device)
    owned = lax.all_to_all(first, "rows", split_axis=1, concat_axis=2, tiled=True)
    mixed = jnp.einsum(
        "ap,bcpq->bcaq",
        c_outer,
        owned.reshape(batches, narrow, outer, INNER),
        precision=lax.Precision.HIGHEST,
    )
    parity = jax.vmap(pair_parity)(samples)
    even_rows = mixed[:, :, :, :halfin].reshape(batches, narrow, half)
    odd_rows = mixed[:, :, :, halfin:].reshape(batches, narrow, half)
    picked = jnp.where(parity[:, None, :] == 1, odd_rows, even_rows)
    rows_back = lax.all_to_all(picked, "rows", split_axis=2, concat_axis=1, tiled=True)
    gram = jnp.einsum("bnr,bmr->nm", rows_back, rows_back, precision=lax.Precision.HIGHEST)
    gram = lax.psum(gram, ("rows", "grp"))
    gram = gram / (ngroups * batches * half)
    lower = jnp.linalg.cholesky(gram)
    inverse = jax.scipy.linalg.solve_triangular(
        lower, jnp.eye(width, dtype=jnp.float32), lower=True
    )
    solved = jnp.dot(
        matrix, inverse.T, precision=lax.Precision.HIGHEST, preferred_element_type=jnp.float32
    )
    return (lower.T, solved)


def solution(mesh):
    placed = (P(("rows", "grp"), None), P(("rows", "grp")), P("grp", None))
    return jax.shard_map(
        local,
        mesh=mesh,
        in_specs=placed,
        out_specs=(P(), P(("rows", "grp"), None)),
        check_vma=False,
    )
```

profile of v0, /device:TPU:2, one launch (start us, length us, event | category | flops | bytes accessed | tf_op | source)
XLA Modules:
  0.0 941.8 jit_solution(5274258557876319001)
XLA Ops:
  10.5 7.6 fusion.30
  18.0 5.4 copy.18
  23.5 12.5 %all-to-all-start = ((f32[4,512,512]{2,0,1:T(4,128)}), f32[4,512,512]{2,0,1:T(4,128)}, u32[]{:S(2)}, u32[]{:S(2)}) async-start(f32[4,512,512]{2,0,1:T(4,128)} %copy.18), calls=%async_computation | async-start | bytes 8388608 | tf_op jit(solution)/shard_map/all_to_all | solution.py:47
  37.3 239.6 %scatter_custom_fusion = s32[65536]{0:T(1024)S(1)} fusion(s32[65536]{0:T(1024)S(1)} %bitcast.107, s32[65536]{0:T(1024)S(1)} %bitcast.108, s32[]{:T(128)} %copy.55), kind=kCustom, calls=%fused_computation.83 | custom fusion | bytes 262148
  285.0 5.2 reshape.110
  290.2 8.8 convolution_bitcast_fusion.1
  310.8 20.2 %copy.24 = f32[4,8,16384]{1,0,2:T(4,128)} copy(f32[4,8,16384]{2,1,0:T(8,128)S(1)} %broadcast_select_fusion) | data formatting | bytes 4194304 | tf_op jit(solution)/shard_map/jit(_where)/select_n | solution.py:57
  330.9 41.0 %reshape.149 = f32[64,1,8192]{2,1,0:T(1,128)S(1)} reshape(f32[16384,4,8]{2,1,0:T(4,128)} %bitcast.102) | data formatting | bytes 4194304
  371.9 62.0 %all_to_all.33 = f32[64,1,8192]{2,1,0:T(1,128)} all-to-all(f32[64,1,8192]{2,1,0:T(1,128)S(1)} %reshape.149), channel_id=1, replica_groups=mesh['rows'=64,'grp'=4] {'rows'}, dimensions={0} | all-to-all | bytes 4194304 | tf_op jit(solution)/shard_map/all_to_all | solution.py:58
  434.4 7.5 reduce.28
  442.0 41.6 %reshape.150 = f32[16384,4,8]{2,1,0:T(4,128)} reshape(f32[64,8192]{1,0:T(8,128)S(1)} %reduce.28) | data formatting | bytes 4194304
  483.6 23.7 %copy.25 = f32[4,8,64,256]{3,1,2,0:T(8,128)S(1)} copy(f32[4,8,64,256]{1,0,3,2:T(4,128)} %bitcast.103) | data formatting | bytes 4194304 | tf_op jit(solution)/shard_map/all_to_all | solution.py:58
  513.0 254.1 %all-reduce.3.cloned.1.call-done = f32[512,512]{0,1:T(8,128)} async-done(((f32[512,512]{0,1:T(8,128)}), f32[512,512]{0,1:T(8,128)}) %all-reduce.3.cloned.1.call-update) | async-done | bytes 1048592 | tf_op jit(solution)/shard_map/psum | solution.py:60
  770.0 11.7 %cholesky.104 = f32[128,128]{1,0:T(8,128)S(1)} custom-call(f32[128,128]{1,0:T(8,128)S(1)} %cholesky.266), custom_call_target="Cholesky" | custom-call | tf_op jit(solution)/shard_map/jit(cholesky)/cholesky | solution.py:62
  781.8 9.8 %custom-call.31 = f32[1,128,128]{1,2,0:T(8,128)S(1)} custom-call(f32[1,128,128]{2,1,0:T(8,128)S(1)} %get-tuple-element.41), custom_call_target="InvertDiagBlocksLowerTriangular" | custom-call | tf_op jit(solution)/shard_map/jit(cholesky)/cholesky | solution.py:62
  794.4 11.9 %cholesky.217 = f32[128,128]{1,0:T(8,128)S(1)} custom-call(f32[128,128]{1,0:T(8,128)S(1)} %cholesky.270), custom_call_target="Cholesky" | custom-call | tf_op jit(solution)/shard_map/jit(cholesky)/cholesky | solution.py:62
  807.7 9.8 %custom-call.32 = f32[1,128,128]{1,2,0:T(8,128)S(1)} custom-call(f32[1,128,128]{2,1,0:T(8,128)S(1)} %get-tuple-element.38), custom_call_target="InvertDiagBlocksLowerTriangular" | custom-call | tf_op jit(solution)/shard_map/jit(cholesky)/cholesky | solution.py:62
  819.0 11.7 %cholesky.238 = f32[128,128]{1,0:T(8,128)S(1)} custom-call(f32[128,128]{1,0:T(8,128)S(1)} %cholesky.275), custom_call_target="Cholesky" | custom-call | tf_op jit(solution)/shard_map/jit(cholesky)/cholesky | solution.py:62
  831.5 9.8 %custom-call.33 = f32[1,128,128]{1,2,0:T(8,128)S(1)} custom-call(f32[1,128,128]{2,1,0:T(8,128)S(1)} %get-tuple-element.35), custom_call_target="InvertDiagBlocksLowerTriangular" | custom-call | tf_op jit(solution)/shard_map/jit(cholesky)/cholesky | solution.py:62
  843.1 11.7 %cholesky.255 = f32[128,128]{1,0:T(8,128)S(1)} custom-call(f32[128,128]{1,0:T(8,128)S(1)} %convolution_subtract_fusion.5), custom_call_target="Cholesky" | custom-call | tf_op jit(solution)/shard_map/jit(cholesky)/cholesky | solution.py:62
  859.3 14.1 %while.1 = (s32[]{:T(128)}, f32[512,512]{1,0:T(8,128)}, s32[4,2]{0,1:T(2,128)S(1)}, f32[4,128,128]{2,1,0:T(8,128)}, s32[]{:T(128)}) while((s32[]{:T(128)}, f32[512,512]{1,0:T(8,128)}, s32[4,2]{0,1:T(2,128)S(1)}, f32[4,128,128]{2,1,0:T(8,128)}, s32[]{:T(128)}) %tuple.37), condition=%wide.while_cond, body=%wide.while_body.sunk | while | flops 2 | bytes 132705 | solution.py:63
  873.4 40.1 %custom-call.34 = f32[4,128,128]{1,2,0:T(8,128)S(1)} custom-call(f32[4,128,128]{2,1,0:T(8,128)} %get-tuple-element.9), custom_call_target="InvertDiagBlocksLowerTriangular" | custom-call | tf_op jit(solution)/shard_map/jit(_solve_triangular)/triangular_solve | solution.py:63
  919.4 8.7 convolution_bitcast_fusion
  928.1 5.3 copy.29
  (90 shorter events, 64.8 us)
Async XLA Ops:
  23.5 12.6 %copy-start.4 = (s32[4,16384]{1,0:T(4,128)S(1)}, s32[4,16384]{1,0:T(4,128)}, u32[]{:S(2)}) copy-start(s32[4,16384]{1,0:T(4,128)} %param.5) | copy-start | bytes 786436
  23.5 13.1 %copy-start.5 = (s32[2]{0:T(128)S(1)}, s32[2]{0:T(128)}, u32[]{:S(2)}) copy-start(s32[2]{0:T(128)} %constant.238) | copy-start | bytes 28
  23.5 13.4 %copy-start.6 = (s32[2]{0:T(128)S(1)}, s32[2]{0:T(128)}, u32[]{:S(2)}) copy-start(s32[2]{0:T(128)} %constant.241) | copy-start | bytes 28
  23.5 253.5 %all-to-all-start = ((f32[4,512,512]{2,0,1:T(4,128)}), f32[4,512,512]{2,0,1:T(4,128)}, u32[]{:S(2)}, u32[]{:S(2)}) async-start(f32[4,512,512]{2,0,1:T(4,128)} %copy.18), calls=%async_computation | async-start | bytes 8388608 | tf_op jit(solution)/shard_map/all_to_all | solution.py:47
  36.0 731.0 %all-reduce.3.cloned.1.call-start = ((), (), s32[]{:S(2)}) async-start(), calls=%async_computation.2 | async-start | bytes 2097152 | tf_op jit(solution)/shard_map/psum | solution.py:60
  767.1 1.8 copy-start.1
  769.1 1.0 copy-start.3
  791.7 122.1 %copy-start.2 = (f32[512,512]{1,0:T(8,128)S(1)}, f32[512,512]{1,0:T(8,128)}, u32[]{:S(2)}) copy-start(f32[512,512]{1,0:T(8,128)} %fusion.23) | copy-start | bytes 3145732
  913.5 5.9 copy-start
Sparse Core Ops, SparseCore 0:
  511.9 255.1 all-reduce.2
where the time goes:
time: 951 us; the launch traced here: 942 us
  local copies, waits for them, and re-layouts  417 us (44%)
  waiting for transfers between devices  254 us (27%)
  other arithmetic  138 us (15%)
  blocking collectives  62 us (7%)
  matrix products  41.3 us (4%)
  between operations  17.2 us (2%)
  starting transfers between devices  12.6 us (1%)
    unnamed x22, local copies, waits for them, and re-layouts  330 us
    psum x1, waiting for transfers between devices, local(): gram = lax.psum(gram, ('rows', 'grp'))  254 us
    another operation x15, other arithmetic, local(): lower = jnp.linalg.cholesky(gram)  79.3 us
    all_to_all x1, blocking collectives, local(): lax.all_to_all(picked, 'rows', split_axis=2, concat_axis=1, tiled=True)  62 us
    another operation x3, other arithmetic, local(): jax.scipy.linalg.solve_triangular(lower, jnp.eye(width, dtype=jnp.float32...  41.4 us
    all_to_all x2, local copies, waits for them, and re-layouts, local(): lax.all_to_all(picked, 'rows', split_axis=2, concat_axis=1, tiled=True)  24.2 us
    select_n x1, local copies, waits for them, and re-layouts, local(): picked = jnp.where(parity[:, None, :] == 1, odd_rows, even_rows)  20.2 us
  transfers between devices with their start and end apart: 2, of which 1 were waited for; matrix products, arithmetic and copies ran while one was open for 26% of the time, Pallas kernels for 0%

commit v1 on v0

--- a/solution.py
+++ b/solution.py
@@ -55,7 +55,10 @@
     even_rows = mixed[:, :, :, :halfin].reshape(batches, narrow, half)
     odd_rows = mixed[:, :, :, halfin:].reshape(batches, narrow, half)
     picked = jnp.where(parity[:, None, :] == 1, odd_rows, even_rows)
-    rows_back = lax.all_to_all(picked, "rows", split_axis=2, concat_axis=1, tiled=True)
+    rows_back = jnp.concatenate(
+        lax.all_to_all(jnp.stack(jnp.split(picked, lax.axis_size("rows"), axis=2)), "rows", 0, 0),
+        axis=1,
+    )
     gram = jnp.einsum("bnr,bmr->nm", rows_back, rows_back, precision=lax.Precision.HIGHEST)
     gram = lax.psum(gram, ("rows", "grp"))
     gram = gram / (ngroups * batches * half)

time: 951 us -> 803 us (0.84)
  local copies, waits for them, and re-layouts: 417 us -> 287 us
    unnamed x22 -> x81, local copies, waits for them, and re-layouts: 330 us -> 247 us
    all_to_all x2 -> x0, local copies, waits for them, and re-layouts: 24.2 us -> none  [local(): lax.all_to_all(picked, 'rows', split_axis=2, concat_axis=1, tiled=True)]
    select_n x1 -> x0, local copies, waits for them, and re-layouts: 20.2 us -> none  [local(): picked = jnp.where(parity[:, None, :] == 1, odd_rows, even_rows)]
  transfers between devices with their start and end apart: 2 -> 2, of which waited for: 1 -> 1; matrix products, arithmetic and copies ran while one was open for 26% -> 30% of each run, Pallas kernels for 0% -> 0%
where the time goes in v1:
time: 803 us; the launch traced here: 796 us
  local copies, waits for them, and re-layouts  287 us (36%)
  waiting for transfers between devices  254 us (32%)
  other arithmetic  129 us (16%)
  blocking collectives  61.4 us (8%)
  matrix products  34.5 us (4%)
  between operations  17.7 us (2%)
  starting transfers between devices  12.5 us (2%)
    psum x1, waiting for transfers between devices, local(): gram = lax.psum(gram, ('rows', 'grp'))  254 us
    unnamed x81, local copies, waits for them, and re-layouts  247 us
    another operation x15, other arithmetic, local(): lower = jnp.linalg.cholesky(gram)  79.6 us
    all_to_all x1, blocking collectives, local(): lax.all_to_all(jnp.stack(jnp.split(picked, lax.axis_size('rows'), axis=2)...  61.4 us
    another operation x3, other arithmetic, local(): jax.scipy.linalg.solve_triangular(lower, jnp.eye(width, dtype=jnp.float32...  40.4 us
  transfers between devices with their start and end apart: 2, of which 1 were waited for; matrix products, arithmetic and copies ran while one was open for 30% of the time, Pallas kernels for 0%

profile of v1, /device:TPU:2, one launch (start us, length us, event | category | flops | bytes accessed | tf_op | source)
XLA Modules:
  0.0 796.5 jit_solution(2821581498170756660)
XLA Ops:
  10.5 7.6 fusion.31
  18.0 5.4 copy.82
  23.5 12.5 %all-to-all-start = ((f32[4,512,512]{2,0,1:T(4,128)}), f32[4,512,512]{2,0,1:T(4,128)}, u32[]{:S(2)}, u32[]{:S(2)}) async-start(f32[4,512,512]{2,0,1:T(4,128)} %copy.82), calls=%async_computation | async-start | bytes 8388608 | tf_op jit(solution)/shard_map/all_to_all | solution.py:47
  37.3 239.7 %scatter_custom_fusion = s32[65536]{0:T(1024)S(1)} fusion(s32[65536]{0:T(1024)S(1)} %bitcast.360, s32[65536]{0:T(1024)S(1)} %bitcast.361, s32[]{:T(128)} %copy.187), kind=kCustom, calls=%fused_computation.148 | custom fusion | bytes 262148
  277.2 3.5 copy.107
  280.8 4.4 copy.84
  285.2 4.9 reshape.116
  290.1 8.8 %convolution_bitcast_fusion.1 = f32[4,8,128,256]{2,3,1,0:T(8,128)S(1)} fusion(f32[4,8,128,256]{3,2,1,0:T(8,128)} %reshape.116, s32[128]{0:T(128)S(1)} %get-tuple-element.45, f32[128]{0:T(128)S(1)} %fusion.88), kind=kOutput, calls=%fused_computation.5 | convolution fusion | flops 1610858496 | bytes 8389632 | tf_op jit(solution)/shard_map/ap,bcpq->bcaq/dot_general | solution.py:48
  304.2 2.9 copy.87
  307.2 2.7 reshape.118
  312.6 61.4 %all_to_all.20 = f32[64,4,8,256]{3,2,1,0:T(8,128)S(1)} all-to-all(f32[64,4,8,256]{3,2,1,0:T(8,128)S(1)} %constant_dynamic-update-slice_fusion), channel_id=1, replica_groups=mesh['rows'=64,'grp'=4] {'rows'}, dimensions={0} | all-to-all | bytes 4194304 | tf_op jit(solution)/shard_map/all_to_all | solution.py:59
  373.9 4.5 fusion.3
  379.7 254.1 %all-reduce.3.cloned.1.call-done = f32[512,512]{0,1:T(8,128)} async-done(((f32[512,512]{0,1:T(8,128)}), f32[512,512]{0,1:T(8,128)}) %all-reduce.3.cloned.1.call-update) | async-done | bytes 1048592 | tf_op jit(solution)/shard_map/psum | solution.py:63
  635.8 11.7 %cholesky.104 = f32[128,128]{1,0:T(8,128)S(1)} custom-call(f32[128,128]{1,0:T(8,128)S(1)} %cholesky.266), custom_call_target="Cholesky" | custom-call | tf_op jit(solution)/shard_map/jit(cholesky)/cholesky | solution.py:65
  647.6 9.8 %custom-call.31 = f32[1,128,128]{1,2,0:T(8,128)S(1)} custom-call(f32[1,128,128]{2,1,0:T(8,128)S(1)} %get-tuple-element.41), custom_call_target="InvertDiagBlocksLowerTriangular" | custom-call | tf_op jit(solution)/shard_map/jit(cholesky)/cholesky | solution.py:65
  658.1 12.1 %cholesky.217 = f32[128,128]{1,0:T(8,128)S(1)} custom-call(f32[128,128]{1,0:T(8,128)S(1)} %cholesky.270), custom_call_target="Cholesky" | custom-call | tf_op jit(solution)/shard_map/jit(cholesky)/cholesky | solution.py:65
  670.3 9.8 %custom-call.32 = f32[1,128,128]{1,2,0:T(8,128)S(1)} custom-call(f32[1,128,128]{2,1,0:T(8,128)S(1)} %get-tuple-element.38), custom_call_target="InvertDiagBlocksLowerTriangular" | custom-call | tf_op jit(solution)/shard_map/jit(cholesky)/cholesky | solution.py:65
  680.8 11.7 %cholesky.238 = f32[128,128]{1,0:T(8,128)S(1)} custom-call(f32[128,128]{1,0:T(8,128)S(1)} %cholesky.275), custom_call_target="Cholesky" | custom-call | tf_op jit(solution)/shard_map/jit(cholesky)/cholesky | solution.py:65
  692.5 9.8 %custom-call.33 = f32[1,128,128]{1,2,0:T(8,128)S(1)} custom-call(f32[1,128,128]{2,1,0:T(8,128)S(1)} %get-tuple-element.35), custom_call_target="InvertDiagBlocksLowerTriangular" | custom-call | tf_op jit(solution)/shard_map/jit(cholesky)/cholesky | solution.py:65
  702.9 11.9 %cholesky.255 = f32[128,128]{1,0:T(8,128)S(1)} custom-call(f32[128,128]{1,0:T(8,128)S(1)} %convolution_subtract_fusion.5), custom_call_target="Cholesky" | custom-call | tf_op jit(solution)/shard_map/jit(cholesky)/cholesky | solution.py:65
  721.6 10.5 %while.1 = (s32[]{:T(128)}, f32[512,512]{1,0:T(8,128)S(1)}, s32[4,2]{0,1:T(2,128)S(1)}, f32[4,128,128]{2,1,0:T(8,128)}, s32[]{:T(128)}) while((s32[]{:T(128)}, f32[512,512]{1,0:T(8,128)S(1)}, s32[4,2]{0,1:T(2,128)S(1)}, f32[4,128,128]{2,1,0:T(8,128)}, s32[]{:T(128)}) %tuple.37), condition=%wide.while_cond, body=%wide.while_body.sunk | while | flops 2 | bytes 132205 | solution.py:66
  732.1 40.1 %custom-call.34 = f32[4,128,128]{1,2,0:T(8,128)S(1)} custom-call(f32[4,128,128]{2,1,0:T(8,128)} %get-tuple-element.9), custom_call_target="InvertDiagBlocksLowerTriangular" | custom-call | tf_op jit(solution)/shard_map/jit(_solve_triangular)/triangular_solve | solution.py:66
  775.4 8.7 %convolution_bitcast_fusion = f32[2048,512]{0,1:T(8,128)} fusion(f32[2048,512]{1,0:T(8,128)S(1)} %copy-done, f32[128,512]{1,0:T(8,128)S(1)} %fusion.65, f32[128,512]{1,0:T(8,128)S(1)} %fusion.66, f32[128,512]{1,0:T(8,128)S(1)} %fusion.68, f32[128,512]{1,0:T(8,128)S(1)} %fusion.37), kind=kOutput, calls=%fused_computation.4 | convolution fusion | flops 6443237376 | bytes 9437184 | tf_op jit(solution)/shard_map/dot_general | solution.py:69
  784.1 5.3 copy.92
  (146 shorter events, 35.2 us)
Async XLA Ops:
  23.5 12.6 %copy-start.3 = (s32[4,16384]{1,0:T(4,128)S(1)}, s32[4,16384]{1,0:T(4,128)}, u32[]{:S(2)}) copy-start(s32[4,16384]{1,0:T(4,128)} %param.5) | copy-start | bytes 786436
  23.5 13.1 %copy-start.4 = (s32[2]{0:T(128)S(1)}, s32[2]{0:T(128)}, u32[]{:S(2)}) copy-start(s32[2]{0:T(128)} %constant.238) | copy-start | bytes 28
  23.5 13.4 %copy-start.5 = (s32[2]{0:T(128)S(1)}, s32[2]{0:T(128)}, u32[]{:S(2)}) copy-start(s32[2]{0:T(128)} %constant.241) | copy-start | bytes 28
  23.5 253.7 %all-to-all-start = ((f32[4,512,512]{2,0,1:T(4,128)}), f32[4,512,512]{2,0,1:T(4,128)}, u32[]{:S(2)}, u32[]{:S(2)}) async-start(f32[4,512,512]{2,0,1:T(4,128)} %copy.82), calls=%async_computation | async-start | bytes 8388608 | tf_op jit(solution)/shard_map/all_to_all | solution.py:47
  36.0 597.7 %all-reduce.3.cloned.1.call-start = ((), (), s32[]{:S(2)}) async-start(), calls=%async_computation.2 | async-start | bytes 2097152 | tf_op jit(solution)/shard_map/psum | solution.py:63
  633.7 1.8 copy-start.1
  720.3 52.3 %copy-start.2 = (f32[512,512]{1,0:T(8,128)S(1)}, f32[512,512]{1,0:T(8,128)}, u32[]{:S(2)}) copy-start(f32[512,512]{1,0:T(8,128)} %fusion.24) | copy-start | bytes 3145732
  773.0 2.4 copy-start
Sparse Core Ops, SparseCore 0:
  378.6 255.0 all-reduce.2
